TPU v7x, 128 devices: a whole 4x4x4 slice. The times are simulated.
128 devices in a mesh: smp: 8 (over x_lo, z), bld: 16 (over y, x_hi, core).
Axes of the slice: x: 4 (x_hi: 2, x_lo: 2; x = x_hi * 2 + x_lo), y: 4, z: 4, core: 2. Of those that a mesh axis runs over, the one named last changes fastest.
Arguments:
- tensor: bfloat16 [4, 8192, 16384], P(None, 'smp', 'bld'), may hold values from -576 to 576
- building_factor: float32 [64, 16384], P(None, 'bld'), may hold values from -144 to 144
- hour_weights: float32 [4, 64], replicated, may hold values from -5 to 5
Outputs:
- sample_factor: float32 [64, 8192], P(None, ('smp', 'bld'))
- building_out: float32 [64, 16384], P(None, ('bld', 'smp'))
- hour_out: float32 [4, 64], replicated
All inputs are finite; a program needn't handle non-finite values.
Results may differ from a plain program's by a relative error of at most 0.008.
Values may be sent and summed in bfloat16 or wider, within the bound.
A program may use at most 64 MiB of HBM per device.

v0:
```python
import math
import jax
import jax.numpy as jnp
from jax import lax
from jax.sharding import PartitionSpec as P

SWEEPS = 5
EPSILON = 1e-06
RIDGE_SHARE = 0.05


def regularized(gram):
    order_size = gram.shape[0]
    return gram + RIDGE_SHARE * jnp.mean(jnp.diagonal(gram)) * jnp.eye(order_size, dtype=gram.dtype)


def solve_rows(gram, right_side):
    lower_factor = jnp.linalg.cholesky(regularized(gram))
    middle = lax.linalg.triangular_solve(lower_factor, right_side, left_side=True, lower=True)
    return lax.linalg.triangular_solve(
        lower_factor, middle, left_side=True, lower=True, transpose_a=True
    )


def finish(unscaled, gram_raw, row_count):
    column_norm = jnp.sqrt(jnp.diagonal(gram_raw) / row_count + EPSILON)
    return (
        unscaled / column_norm[:, None],
        gram_raw / (column_norm[:, None] * column_norm[None, :]),
    )


def hour_gram(hourly):
    return jnp.dot(hourly.T, hourly, precision=lax.Precision.HIGHEST)


def self_gram(unscaled):
    return jnp.dot(unscaled, unscaled.T, precision=lax.Precision.HIGHEST)


def local(tensor, building_factor, hour_weights):
    samples_total = tensor.shape[1] * lax.axis_size("smp")
    buildings_total = tensor.shape[2] * lax.axis_size("bld")
    scale_up = math.sqrt(samples_total * buildings_total)
    hourly = hour_weights / scale_up
    gram_build = lax.psum(self_gram(building_factor), "bld")
    build_low = building_factor.astype(jnp.bfloat16)
    partial_value = jnp.einsum("rj,kij->kri", build_low, tensor, preferred_element_type=jnp.float32)
    sample_out = None
    building_out = None
    for sweep_index in range(SWEEPS):
        sample_terms = jnp.sum(hourly[:, :, None] * partial_value, axis=0)
        sample_rhs = lax.psum(sample_terms, "bld")
        unscaled = solve_rows(gram_build * hour_gram(hourly), sample_rhs)
        gram_raw = lax.psum(self_gram(unscaled), "smp")
        samples_now, gram_sample = finish(unscaled, gram_raw, samples_total)
        sample_low = samples_now.astype(jnp.bfloat16)
        share_width = samples_now.shape[1] // lax.axis_size("bld")
        sample_out = lax.dynamic_slice_in_dim(
            samples_now, lax.axis_index("bld") * share_width, share_width, 1
        )
        mixed = jnp.einsum("ri,kij->krj", sample_low, tensor, preferred_element_type=jnp.float32)
        build_terms = jnp.sum(hourly[:, :, None] * mixed, axis=0)
        build_rhs = lax.psum(build_terms, "smp")
        unscaled = solve_rows(gram_sample * hour_gram(hourly), build_rhs)
        gram_raw = lax.psum(self_gram(unscaled), "bld")
        building_now, gram_build = finish(unscaled, gram_raw, buildings_total)
        build_low = building_now.astype(jnp.bfloat16)
        share_width = building_now.shape[1] // lax.axis_size("smp")
        building_out = lax.dynamic_slice_in_dim(
            building_now, lax.axis_index("smp") * share_width, share_width, 1
        )
        partial_value = jnp.einsum(
            "rj,kij->kri", build_low, tensor, preferred_element_type=jnp.float32
        )
        hour_terms = jnp.sum(sample_low.astype(jnp.float32)[None, :, :] * partial_value, axis=2)
        hour_rhs = lax.psum(hour_terms, ("smp", "bld"))
        hourly = solve_rows(gram_sample * gram_build, hour_rhs.T).T
    return (sample_out, building_out, hourly * scale_up)


def solution(mesh):
    in_specs = (P(None, "smp", "bld"), P(None, "bld"), P())
    out_specs = (P(None, ("smp", "bld")), P(None, ("bld", "smp")), P())
    return jax.shard_map(local, mesh=mesh, in_specs=in_specs, out_specs=out_specs, check_vma=False)
```

profile of v0, /device:TPU:1, one launch (start us, length us, event | category | flops | bytes accessed | tf_op | source)
XLA Modules:
  0.0 2094.5 jit_solution(17855161390660669668)
XLA Ops:
  8.0 6.7 fusion.10
  15.2 65.3 %psum.182 = f32[64,64]{0,1:T(8,128)S(1)} all-reduce(f32[64,64]{0,1:T(8,128)S(1)} %fusion.159), channel_id=1, replica_groups=mesh['smp'=8,'bld'=16] {'bld'}, use_global_device_ids=true, to_apply=%region_0.0 | all-reduce | flops 4096 | bytes 32768 | tf_op jit(solution)/shard_map/psum | solution.py:46
  82.9 5.8 cholesky.239
  95.0 60.6 %all-reduce.11.cloned.1.call-done = f32[64,1024]{1,0:T(8,128)} async-done(((f32[64,1024]{1,0:T(8,128)}), f32[64,1024]{1,0:T(8,128)}) %all-reduce.11.cloned.1.call-update) | async-done | bytes 262160 | tf_op jit(solution)/shard_map/psum | solution.py:53
  157.7 26.2 %psum.184 = f32[64,64]{0,1:T(8,128)S(1)} all-reduce(f32[64,64]{0,1:T(8,128)S(1)} %fusion.160), channel_id=1, replica_groups=mesh['smp'=8,'bld'=16] {'smp'}, use_global_device_ids=true, to_apply=%region_6.10 | all-reduce | flops 4096 | bytes 32768 | tf_op jit(solution)/shard_map/psum | solution.py:55
  192.8 5.8 cholesky.250
  205.1 65.8 %all-reduce.13.cloned.1.call-done = f32[64,1024]{1,0:T(8,128)} async-done(((f32[64,1024]{1,0:T(8,128)}), f32[64,1024]{1,0:T(8,128)}) %all-reduce.13.cloned.1.call-update) | async-done | bytes 262160 | tf_op jit(solution)/shard_map/psum | solution.py:64
  273.0 65.3 %psum.186 = f32[64,64]{0,1:T(8,128)S(1)} all-reduce(f32[64,64]{0,1:T(8,128)S(1)} %fusion.161), channel_id=1, replica_groups=mesh['smp'=8,'bld'=16] {'bld'}, use_global_device_ids=true, to_apply=%region_10.14 | all-reduce | flops 4096 | bytes 32768 | tf_op jit(solution)/shard_map/psum | solution.py:66
  341.4 5.8 cholesky.261
  353.5 6.2 multiply_reduce_fusion.7
  359.6 67.3 %psum.187 = f32[64,4]{0,1:T(4,128)S(1)} all-reduce(f32[64,4]{0,1:T(4,128)S(1)} %bitcast.367), channel_id=1, replica_groups=mesh['smp'=8,'bld'=16] {'smp','bld'}, use_global_device_ids=true, to_apply=%region_13.17 | all-reduce | flops 256 | bytes 2048 | tf_op jit(solution)/shard_map/psum | solution.py:77
  429.7 5.8 cholesky.272
  442.7 127.8 %all-reduce.15.cloned.1.call-done = f32[64,1024]{1,0:T(8,128)} async-done(((f32[64,1024]{1,0:T(8,128)}), f32[64,1024]{1,0:T(8,128)}) %all-reduce.15.cloned.1.call-update) | async-done | bytes 262160 | tf_op jit(solution)/shard_map/psum | solution.py:53
  572.6 26.5 %psum.189 = f32[64,64]{0,1:T(8,128)S(1)} all-reduce(f32[64,64]{0,1:T(8,128)S(1)} %fusion.162), channel_id=1, replica_groups=mesh['smp'=8,'bld'=16] {'smp'}, use_global_device_ids=true, to_apply=%region_17.23 | all-reduce | flops 4096 | bytes 32768 | tf_op jit(solution)/shard_map/psum | solution.py:55
  607.9 5.8 cholesky.283
  620.2 65.8 %all-reduce.17.cloned.1.call-done = f32[64,1024]{1,0:T(8,128)} async-done(((f32[64,1024]{1,0:T(8,128)}), f32[64,1024]{1,0:T(8,128)}) %all-reduce.17.cloned.1.call-update) | async-done | bytes 262160 | tf_op jit(solution)/shard_map/psum | solution.py:64
  688.1 64.7 %psum.191 = f32[64,64]{0,1:T(8,128)S(1)} all-reduce(f32[64,64]{0,1:T(8,128)S(1)} %fusion.163), channel_id=1, replica_groups=mesh['smp'=8,'bld'=16] {'bld'}, use_global_device_ids=true, to_apply=%region_21.27 | all-reduce | flops 4096 | bytes 32768 | tf_op jit(solution)/shard_map/psum | solution.py:66
  755.9 5.8 cholesky.294
  768.0 6.2 multiply_reduce_fusion.5
  774.2 67.5 %psum.192 = f32[64,4]{0,1:T(4,128)S(1)} all-reduce(f32[64,4]{0,1:T(4,128)S(1)} %bitcast.368), channel_id=1, replica_groups=mesh['smp'=8,'bld'=16] {'smp','bld'}, use_global_device_ids=true, to_apply=%region_24.30 | all-reduce | flops 256 | bytes 2048 | tf_op jit(solution)/shard_map/psum | solution.py:77
  844.5 5.8 cholesky.305
  857.5 127.8 %all-reduce.19.cloned.1.call-done = f32[64,1024]{1,0:T(8,128)} async-done(((f32[64,1024]{1,0:T(8,128)}), f32[64,1024]{1,0:T(8,128)}) %all-reduce.19.cloned.1.call-update) | async-done | bytes 262160 | tf_op jit(solution)/shard_map/psum | solution.py:53
  987.4 26.2 %psum.194 = f32[64,64]{0,1:T(8,128)S(1)} all-reduce(f32[64,64]{0,1:T(8,128)S(1)} %fusion.164), channel_id=1, replica_groups=mesh['smp'=8,'bld'=16] {'smp'}, use_global_device_ids=true, to_apply=%region_28.34 | all-reduce | flops 4096 | bytes 32768 | tf_op jit(solution)/shard_map/psum | solution.py:55
  1022.4 5.8 cholesky.316
  1034.7 65.8 %all-reduce.21.cloned.1.call-done = f32[64,1024]{1,0:T(8,128)} async-done(((f32[64,1024]{1,0:T(8,128)}), f32[64,1024]{1,0:T(8,128)}) %all-reduce.21.cloned.1.call-update) | async-done | bytes 262160 | tf_op jit(solution)/shard_map/psum | solution.py:64
  1102.6 65.2 %psum.196 = f32[64,64]{0,1:T(8,128)S(1)} all-reduce(f32[64,64]{0,1:T(8,128)S(1)} %fusion.165), channel_id=1, replica_groups=mesh['smp'=8,'bld'=16] {'bld'}, use_global_device_ids=true, to_apply=%region_32.38 | all-reduce | flops 4096 | bytes 32768 | tf_op jit(solution)/shard_map/psum | solution.py:66
  1170.8 5.8 cholesky.327
  1182.9 6.2 multiply_reduce_fusion.3
  1189.1 67.3 %psum.197 = f32[64,4]{0,1:T(4,128)S(1)} all-reduce(f32[64,4]{0,1:T(4,128)S(1)} %bitcast.369), channel_id=1, replica_groups=mesh['smp'=8,'bld'=16] {'smp','bld'}, use_global_device_ids=true, to_apply=%region_35.41 | all-reduce | flops 256 | bytes 2048 | tf_op jit(solution)/shard_map/psum | solution.py:77
  1259.2 5.8 cholesky.338
  1272.2 127.8 %all-reduce.23.cloned.1.call-done = f32[64,1024]{1,0:T(8,128)} async-done(((f32[64,1024]{1,0:T(8,128)}), f32[64,1024]{1,0:T(8,128)}) %all-reduce.23.cloned.1.call-update) | async-done | bytes 262160 | tf_op jit(solution)/shard_map/psum | solution.py:53
  1402.0 26.5 %psum.199 = f32[64,64]{0,1:T(8,128)S(1)} all-reduce(f32[64,64]{0,1:T(8,128)S(1)} %fusion.166), channel_id=1, replica_groups=mesh['smp'=8,'bld'=16] {'smp'}, use_global_device_ids=true, to_apply=%region_39.45 | all-reduce | flops 4096 | bytes 32768 | tf_op jit(solution)/shard_map/psum | solution.py:55
  1429.4 5.8 fusion.8
  1437.4 5.8 cholesky.349
  1449.7 65.8 %all-reduce.25.cloned.1.call-done = f32[64,1024]{1,0:T(8,128)} async-done(((f32[64,1024]{1,0:T(8,128)}), f32[64,1024]{1,0:T(8,128)}) %all-reduce.25.cloned.1.call-update) | async-done | bytes 262160 | tf_op jit(solution)/shard_map/psum | solution.py:64
  1517.6 64.7 %psum.201 = f32[64,64]{0,1:T(8,128)S(1)} all-reduce(f32[64,64]{0,1:T(8,128)S(1)} %fusion.167), channel_id=1, replica_groups=mesh['smp'=8,'bld'=16] {'bld'}, use_global_device_ids=true, to_apply=%region_43.49 | all-reduce | flops 4096 | bytes 32768 | tf_op jit(solution)/shard_map/psum | solution.py:66
  1585.4 5.8 cholesky.360
  1597.5 6.2 multiply_reduce_fusion.1
  1603.6 67.5 %psum.202 = f32[64,4]{0,1:T(4,128)S(1)} all-reduce(f32[64,4]{0,1:T(4,128)S(1)} %bitcast.370), channel_id=1, replica_groups=mesh['smp'=8,'bld'=16] {'smp','bld'}, use_global_device_ids=true, to_apply=%region_46.52 | all-reduce | flops 256 | bytes 2048 | tf_op jit(solution)/shard_map/psum | solution.py:77
  1673.9 5.8 cholesky.371
  1686.9 127.8 %all-reduce.27.cloned.1.call-done = f32[64,1024]{1,0:T(8,128)} async-done(((f32[64,1024]{1,0:T(8,128)}), f32[64,1024]{1,0:T(8,128)}) %all-reduce.27.cloned.1.call-update) | async-done | bytes 262160 | tf_op jit(solution)/shard_map/psum | solution.py:53
  1816.8 26.2 %psum.204 = f32[64,64]{0,1:T(8,128)S(1)} all-reduce(f32[64,64]{0,1:T(8,128)S(1)} %fusion.168), channel_id=1, replica_groups=mesh['smp'=8,'bld'=16] {'smp'}, use_global_device_ids=true, to_apply=%region_50.56 | all-reduce | flops 4096 | bytes 32768 | tf_op jit(solution)/shard_map/psum | solution.py:55
  1846.2 5.8 cholesky.382
  1864.7 65.3 %all-reduce.29.cloned.1.call-done = f32[64,1024]{1,0:T(8,128)} async-done(((f32[64,1024]{1,0:T(8,128)}), f32[64,1024]{1,0:T(8,128)}) %all-reduce.29.cloned.1.call-update) | async-done | bytes 262160 | tf_op jit(solution)/shard_map/psum | solution.py:64
  1932.1 65.0 %psum.206 = f32[64,64]{0,1:T(8,128)S(1)} all-reduce(f32[64,64]{0,1:T(8,128)S(1)} %fusion.169), channel_id=1, replica_groups=mesh['smp'=8,'bld'=16] {'bld'}, use_global_device_ids=true, to_apply=%region_54.60 | all-reduce | flops 4096 | bytes 32768 | tf_op jit(solution)/shard_map/psum | solution.py:66
  2000.3 5.8 cholesky.393
  2012.4 6.2 fusion.11
  2018.5 67.3 %psum.207 = f32[64,4]{0,1:T(4,128)S(1)} all-reduce(f32[64,4]{0,1:T(4,128)S(1)} %fusion.11), channel_id=1, replica_groups=mesh['smp'=8,'bld'=16] {'smp','bld'}, use_global_device_ids=true, to_apply=%region_57.63 | all-reduce | flops 256 | bytes 2048 | tf_op jit(solution)/shard_map/psum | solution.py:77
  (253 shorter events, 179.2 us)
Async XLA Ops:
  7.2 73.3 %copy-start.1 = (f32[4,64]{1,0:T(4,128)S(1)}, f32[4,64]{1,0:T(4,128)}, u32[]{:S(2)}) copy-start(f32[4,64]{1,0:T(4,128)} %param.14) | copy-start | bytes 3076
  7.2 7.6 copy-start
  7.2 148.4 %all-reduce.11.cloned.1.call-start = ((), (), s32[]{:S(2)}) async-start(), calls=%async_computation | async-start | bytes 524288 | tf_op jit(solution)/shard_map/psum | solution.py:53
  14.7 256.2 %all-reduce.13.cloned.1.call-start = ((), (), s32[]{:S(2)}) async-start(), calls=%async_computation.1 | async-start | bytes 524288 | tf_op jit(solution)/shard_map/psum | solution.py:64
  199.4 371.1 %all-reduce.15.cloned.1.call-start = ((), (), s32[]{:S(2)}) async-start(), calls=%async_computation.2 | async-start | bytes 524288 | tf_op jit(solution)/shard_map/psum | solution.py:53
  436.5 249.5 %all-reduce.17.cloned.1.call-start = ((), (), s32[]{:S(2)}) async-start(), calls=%async_computation.3 | async-start | bytes 524288 | tf_op jit(solution)/shard_map/psum | solution.py:64
  614.5 370.8 %all-reduce.19.cloned.1.call-start = ((), (), s32[]{:S(2)}) async-start(), calls=%async_computation.4 | async-start | bytes 524288 | tf_op jit(solution)/shard_map/psum | solution.py:53
  851.2 249.2 %all-reduce.21.cloned.1.call-start = ((), (), s32[]{:S(2)}) async-start(), calls=%async_computation.5 | async-start | bytes 524288 | tf_op jit(solution)/shard_map/psum | solution.py:64
  1029.0 371.0 %all-reduce.23.cloned.1.call-start = ((), (), s32[]{:S(2)}) async-start(), calls=%async_computation.6 | async-start | bytes 524288 | tf_op jit(solution)/shard_map/psum | solution.py:53
  1265.9 249.5 %all-reduce.25.cloned.1.call-start = ((), (), s32[]{:S(2)}) async-start(), calls=%async_computation.7 | async-start | bytes 524288 | tf_op jit(solution)/shard_map/psum | solution.py:64
  1443.9 370.8 %all-reduce.27.cloned.1.call-start = ((), (), s32[]{:S(2)}) async-start(), calls=%async_computation.8 | async-start | bytes 524288 | tf_op jit(solution)/shard_map/psum | solution.py:53
  1680.7 249.3 %all-reduce.29.cloned.1.call-start = ((), (), s32[]{:S(2)}) async-start(), calls=%async_computation.9 | async-start | bytes 524288 | tf_op jit(solution)/shard_map/psum | solution.py:64
Sparse Core Ops, SparseCore 0:
  14.8 140.7 all-reduce.10
  199.5 71.3 all-reduce.12
  436.6 133.8 all-reduce.14
  614.6 71.3 all-reduce.16
  851.4 133.8 all-reduce.18
  1029.1 71.3 all-reduce.20
  1266.0 133.8 all-reduce.22
  1444.1 71.3 all-reduce.24
  1680.8 133.8 all-reduce.26
  1858.6 71.3 all-reduce.28
where the time goes:
time: 2100 us; the launch traced here: 2090 us
  waiting for transfers between devices  900 us (43%)
  blocking collectives  859 us (41%)
  other arithmetic  196 us (9%)
  matrix products  90.9 us (4%)
  between operations  25.1 us (1%)
  local copies, waits for them, and re-layouts  22.6 us (1%)
    psum x5, waiting for transfers between devices, local(): sample_rhs = lax.psum(sample_terms, 'bld')  572 us
    psum x5, blocking collectives, local(): hour_rhs = lax.psum(hour_terms, ('smp', 'bld'))  337 us
    psum x5, waiting for transfers between devices, local(): build_rhs = lax.psum(build_terms, 'smp')  328 us
    psum x5, blocking collectives, local(): gram_raw = lax.psum(self_gram(unscaled), 'bld')  325 us
    psum x5, blocking collectives, local(): gram_raw = lax.psum(self_gram(unscaled), 'smp')  132 us
    another operation x45, other arithmetic, solve_rows(): lower_factor = jnp.linalg.cholesky(regularized(gram))  97.7 us
    another operation x30, other arithmetic, solve_rows(): lax.linalg.triangular_solve(lower_factor, middle, left_side=True, lower=T...  83.3 us
    psum x1, blocking collectives, local(): gram_build = lax.psum(self_gram(building_factor), 'bld')  65.3 us
  transfers between devices with their start and end apart: 10, of which 10 were waited for; matrix products, arithmetic and copies ran while one was open for 3% of the time, Pallas kernels for 0%

commit v1 on v0

--- a/solution.py
+++ b/solution.py
@@ -74,7 +74,10 @@
             "rj,kij->kri", build_low, tensor, preferred_element_type=jnp.float32
         )
         hour_terms = jnp.sum(sample_low.astype(jnp.float32)[None, :, :] * partial_value, axis=2)
-        hour_rhs = lax.psum(hour_terms, ("smp", "bld"))
+        _build_shapes = lambda my_data: lax.psum(
+            lax.psum(my_data, axis_name="bld"), axis_name="smp"
+        )
+        hour_rhs = _build_shapes(hour_terms)
         hourly = solve_rows(gram_sample * gram_build, hour_rhs.T).T
     return (sample_out, building_out, hourly * scale_up)
 

time: 2100 us -> 2030 us (0.967)
  blocking collectives: 859 us -> 782 us
    psum x5 -> x10, blocking collectives: 337 us -> 261 us  [the longest x5 192 us: local(): lax.psum(my_data, axis_name='bld')]
where the time goes in v1:
time: 2030 us; the launch traced here: 2020 us
  waiting for transfers between devices  903 us (44%)
  blocking collectives  782 us (39%)
  other arithmetic  196 us (10%)
  matrix products  90.9 us (4%)
  between operations  25.4 us (1%)
  local copies, waits for them, and re-layouts  22.6 us (1%)
    psum x5, waiting for transfers between devices, local(): sample_rhs = lax.psum(sample_terms, 'bld')  575 us
    psum x5, waiting for transfers between devices, local(): build_rhs = lax.psum(build_terms, 'smp')  328 us
    psum x5, blocking collectives, local(): gram_raw = lax.psum(self_gram(unscaled), 'bld')  324 us
    psum x5, blocking collectives, local(): lax.psum(my_data, axis_name='bld')  192 us
    psum x5, blocking collectives, local(): gram_raw = lax.psum(self_gram(unscaled), 'smp')  132 us
    another operation x45, other arithmetic, solve_rows(): lower_factor = jnp.linalg.cholesky(regularized(gram))  97.7 us
    another operation x30, other arithmetic, solve_rows(): lax.linalg.triangular_solve(lower_factor, middle, left_side=True, lower=T...  83.3 us
    psum x5, blocking collectives, local(): lax.psum(lax.psum(my_data, axis_name='bld'), axis_name='smp')  68.9 us
  transfers between devices with their start and end apart: 10, of which 10 were waited for; matrix products, arithmetic and copies ran while one was open for 3% of the time, Pallas kernels for 0%

profile of v1, /device:TPU:1, one launch (start us, length us, event | category | flops | bytes accessed | tf_op | source)
XLA Modules:
  0.0 2021.1 jit_solution(6296704623136235630)
XLA Ops:
  8.0 6.7 fusion.10
  15.2 65.3 %psum.217 = f32[64,64]{0,1:T(8,128)S(1)} all-reduce(f32[64,64]{0,1:T(8,128)S(1)} %fusion.159), channel_id=1, replica_groups=mesh['smp'=8,'bld'=16] {'bld'}, use_global_device_ids=true, to_apply=%region_0.0 | all-reduce | flops 4096 | bytes 32768 | tf_op jit(solution)/shard_map/psum | solution.py:46
  82.9 5.8 cholesky.239
  95.0 60.6 %all-reduce.11.cloned.1.call-done = f32[64,1024]{1,0:T(8,128)} async-done(((f32[64,1024]{1,0:T(8,128)}), f32[64,1024]{1,0:T(8,128)}) %all-reduce.11.cloned.1.call-update) | async-done | bytes 262160 | tf_op jit(solution)/shard_map/psum | solution.py:53
  157.7 26.2 %psum.219 = f32[64,64]{0,1:T(8,128)S(1)} all-reduce(f32[64,64]{0,1:T(8,128)S(1)} %fusion.160), channel_id=1, replica_groups=mesh['smp'=8,'bld'=16] {'smp'}, use_global_device_ids=true, to_apply=%region_6.10 | all-reduce | flops 4096 | bytes 32768 | tf_op jit(solution)/shard_map/psum | solution.py:55
  192.8 5.8 cholesky.250
  205.1 65.8 %all-reduce.13.cloned.1.call-done = f32[64,1024]{1,0:T(8,128)} async-done(((f32[64,1024]{1,0:T(8,128)}), f32[64,1024]{1,0:T(8,128)}) %all-reduce.13.cloned.1.call-update) | async-done | bytes 262160 | tf_op jit(solution)/shard_map/psum | solution.py:64
  273.0 65.0 %psum.221 = f32[64,64]{0,1:T(8,128)S(1)} all-reduce(f32[64,64]{0,1:T(8,128)S(1)} %fusion.161), channel_id=1, replica_groups=mesh['smp'=8,'bld'=16] {'bld'}, use_global_device_ids=true, to_apply=%region_10.14 | all-reduce | flops 4096 | bytes 32768 | tf_op jit(solution)/shard_map/psum | solution.py:66
  341.1 5.8 cholesky.261
  353.2 6.2 multiply_reduce_fusion.7
  359.3 38.4 %psum.222 = f32[4,64]{1,0:T(4,128)S(1)} all-reduce(f32[4,64]{1,0:T(4,128)S(1)} %get-tuple-element.12), channel_id=1, replica_groups=mesh['smp'=8,'bld'=16] {'bld'}, use_global_device_ids=true, to_apply=%region_13.17 | all-reduce | flops 256 | bytes 2048 | tf_op jit(solution)/shard_map/psum | solution.py:78
  397.7 13.7 psum.223
  414.2 5.8 cholesky.272
  427.2 128.6 %all-reduce.15.cloned.1.call-done = f32[64,1024]{1,0:T(8,128)} async-done(((f32[64,1024]{1,0:T(8,128)}), f32[64,1024]{1,0:T(8,128)}) %all-reduce.15.cloned.1.call-update) | async-done | bytes 262160 | tf_op jit(solution)/shard_map/psum | solution.py:53
  557.9 26.2 %psum.225 = f32[64,64]{0,1:T(8,128)S(1)} all-reduce(f32[64,64]{0,1:T(8,128)S(1)} %fusion.162), channel_id=1, replica_groups=mesh['smp'=8,'bld'=16] {'smp'}, use_global_device_ids=true, to_apply=%region_18.24 | all-reduce | flops 4096 | bytes 32768 | tf_op jit(solution)/shard_map/psum | solution.py:55
  593.0 5.8 cholesky.283
  605.7 65.4 %all-reduce.17.cloned.1.call-done = f32[64,1024]{1,0:T(8,128)} async-done(((f32[64,1024]{1,0:T(8,128)}), f32[64,1024]{1,0:T(8,128)}) %all-reduce.17.cloned.1.call-update) | async-done | bytes 262160 | tf_op jit(solution)/shard_map/psum | solution.py:64
  673.2 64.7 %psum.227 = f32[64,64]{0,1:T(8,128)S(1)} all-reduce(f32[64,64]{0,1:T(8,128)S(1)} %fusion.163), channel_id=1, replica_groups=mesh['smp'=8,'bld'=16] {'bld'}, use_global_device_ids=true, to_apply=%region_22.28 | all-reduce | flops 4096 | bytes 32768 | tf_op jit(solution)/shard_map/psum | solution.py:66
  741.0 5.8 cholesky.294
  753.1 6.2 multiply_reduce_fusion.5
  759.2 38.4 %psum.228 = f32[4,64]{1,0:T(4,128)S(1)} all-reduce(f32[4,64]{1,0:T(4,128)S(1)} %get-tuple-element.16), channel_id=1, replica_groups=mesh['smp'=8,'bld'=16] {'bld'}, use_global_device_ids=true, to_apply=%region_25.31 | all-reduce | flops 256 | bytes 2048 | tf_op jit(solution)/shard_map/psum | solution.py:78
  797.6 13.7 psum.229
  814.1 5.8 cholesky.305
  827.1 128.8 %all-reduce.19.cloned.1.call-done = f32[64,1024]{1,0:T(8,128)} async-done(((f32[64,1024]{1,0:T(8,128)}), f32[64,1024]{1,0:T(8,128)}) %all-reduce.19.cloned.1.call-update) | async-done | bytes 262160 | tf_op jit(solution)/shard_map/psum | solution.py:53
  958.0 26.5 %psum.231 = f32[64,64]{0,1:T(8,128)S(1)} all-reduce(f32[64,64]{0,1:T(8,128)S(1)} %fusion.164), channel_id=1, replica_groups=mesh['smp'=8,'bld'=16] {'smp'}, use_global_device_ids=true, to_apply=%region_30.36 | all-reduce | flops 4096 | bytes 32768 | tf_op jit(solution)/shard_map/psum | solution.py:55
  993.4 5.8 cholesky.316
  1005.7 65.8 %all-reduce.21.cloned.1.call-done = f32[64,1024]{1,0:T(8,128)} async-done(((f32[64,1024]{1,0:T(8,128)}), f32[64,1024]{1,0:T(8,128)}) %all-reduce.21.cloned.1.call-update) | async-done | bytes 262160 | tf_op jit(solution)/shard_map/psum | solution.py:64
  1073.6 64.7 %psum.233 = f32[64,64]{0,1:T(8,128)S(1)} all-reduce(f32[64,64]{0,1:T(8,128)S(1)} %fusion.165), channel_id=1, replica_groups=mesh['smp'=8,'bld'=16] {'bld'}, use_global_device_ids=true, to_apply=%region_34.40 | all-reduce | flops 4096 | bytes 32768 | tf_op jit(solution)/shard_map/psum | solution.py:66
  1141.4 5.8 cholesky.327
  1153.5 6.2 multiply_reduce_fusion.3
  1159.6 38.4 %psum.234 = f32[4,64]{1,0:T(4,128)S(1)} all-reduce(f32[4,64]{1,0:T(4,128)S(1)} %get-tuple-element.20), channel_id=1, replica_groups=mesh['smp'=8,'bld'=16] {'bld'}, use_global_device_ids=true, to_apply=%region_37.43 | all-reduce | flops 256 | bytes 2048 | tf_op jit(solution)/shard_map/psum | solution.py:78
  1198.0 13.7 psum.235
  1214.5 5.8 cholesky.338
  1227.7 128.4 %all-reduce.23.cloned.1.call-done = f32[64,1024]{1,0:T(8,128)} async-done(((f32[64,1024]{1,0:T(8,128)}), f32[64,1024]{1,0:T(8,128)}) %all-reduce.23.cloned.1.call-update) | async-done | bytes 262160 | tf_op jit(solution)/shard_map/psum | solution.py:53
  1358.2 26.2 %psum.237 = f32[64,64]{0,1:T(8,128)S(1)} all-reduce(f32[64,64]{0,1:T(8,128)S(1)} %fusion.166), channel_id=1, replica_groups=mesh['smp'=8,'bld'=16] {'smp'}, use_global_device_ids=true, to_apply=%region_42.48 | all-reduce | flops 4096 | bytes 32768 | tf_op jit(solution)/shard_map/psum | solution.py:55
  1393.3 5.8 cholesky.349
  1405.6 65.8 %all-reduce.25.cloned.1.call-done = f32[64,1024]{1,0:T(8,128)} async-done(((f32[64,1024]{1,0:T(8,128)}), f32[64,1024]{1,0:T(8,128)}) %all-reduce.25.cloned.1.call-update) | async-done | bytes 262160 | tf_op jit(solution)/shard_map/psum | solution.py:64
  1473.4 64.7 %psum.239 = f32[64,64]{0,1:T(8,128)S(1)} all-reduce(f32[64,64]{0,1:T(8,128)S(1)} %fusion.167), channel_id=1, replica_groups=mesh['smp'=8,'bld'=16] {'bld'}, use_global_device_ids=true, to_apply=%region_46.52 | all-reduce | flops 4096 | bytes 32768 | tf_op jit(solution)/shard_map/psum | solution.py:66
  1553.3 6.2 multiply_reduce_fusion.1
  1559.5 38.4 %psum.240 = f32[4,64]{1,0:T(4,128)S(1)} all-reduce(f32[4,64]{1,0:T(4,128)S(1)} %get-tuple-element.24), channel_id=1, replica_groups=mesh['smp'=8,'bld'=16] {'bld'}, use_global_device_ids=true, to_apply=%region_49.55 | all-reduce | flops 256 | bytes 2048 | tf_op jit(solution)/shard_map/psum | solution.py:78
  1597.9 14.0 psum.241
  1627.6 128.6 %all-reduce.27.cloned.1.call-done = f32[64,1024]{1,0:T(8,128)} async-done(((f32[64,1024]{1,0:T(8,128)}), f32[64,1024]{1,0:T(8,128)}) %all-reduce.27.cloned.1.call-update) | async-done | bytes 262160 | tf_op jit(solution)/shard_map/psum | solution.py:53
  1758.4 26.5 %psum.243 = f32[64,64]{0,1:T(8,128)S(1)} all-reduce(f32[64,64]{0,1:T(8,128)S(1)} %fusion.168), channel_id=1, replica_groups=mesh['smp'=8,'bld'=16] {'smp'}, use_global_device_ids=true, to_apply=%region_54.60 | all-reduce | flops 4096 | bytes 32768 | tf_op jit(solution)/shard_map/psum | solution.py:55
  1806.7 64.9 %all-reduce.29.cloned.1.call-done = f32[64,1024]{1,0:T(8,128)} async-done(((f32[64,1024]{1,0:T(8,128)}), f32[64,1024]{1,0:T(8,128)}) %all-reduce.29.cloned.1.call-update) | async-done | bytes 262160 | tf_op jit(solution)/shard_map/psum | solution.py:64
  1873.7 65.0 %psum.245 = f32[64,64]{0,1:T(8,128)S(1)} all-reduce(f32[64,64]{0,1:T(8,128)S(1)} %fusion.169), channel_id=1, replica_groups=mesh['smp'=8,'bld'=16] {'bld'}, use_global_device_ids=true, to_apply=%region_58.64 | all-reduce | flops 4096 | bytes 32768 | tf_op jit(solution)/shard_map/psum | solution.py:66
  1954.0 6.2 fusion.11
  1960.1 38.4 %psum.246 = f32[4,64]{1,0:T(4,128)S(1)} all-reduce(f32[4,64]{1,0:T(4,128)S(1)} %bitcast.369), channel_id=1, replica_groups=mesh['smp'=8,'bld'=16] {'bld'}, use_global_device_ids=true, to_apply=%region_61.67 | all-reduce | flops 256 | bytes 2048 | tf_op jit(solution)/shard_map/psum | solution.py:78
  1998.5 13.7 psum.247
  (258 shorter events, 208.9 us)
Async XLA Ops:
  7.2 73.3 %copy-start.1 = (f32[4,64]{1,0:T(4,128)S(1)}, f32[4,64]{1,0:T(4,128)}, u32[]{:S(2)}) copy-start(f32[4,64]{1,0:T(4,128)} %param.14) | copy-start | bytes 3076
  7.2 7.6 copy-start
  7.2 148.4 %all-reduce.11.cloned.1.call-start = ((), (), s32[]{:S(2)}) async-start(), calls=%async_computation | async-start | bytes 524288 | tf_op jit(solution)/shard_map/psum | solution.py:53
  14.7 256.2 %all-reduce.13.cloned.1.call-start = ((), (), s32[]{:S(2)}) async-start(), calls=%async_computation.1 | async-start | bytes 524288 | tf_op jit(solution)/shard_map/psum | solution.py:64
  199.4 356.5 %all-reduce.15.cloned.1.call-start = ((), (), s32[]{:S(2)}) async-start(), calls=%async_computation.2 | async-start | bytes 524288 | tf_op jit(solution)/shard_map/psum | solution.py:53
  421.0 250.1 %all-reduce.17.cloned.1.call-start = ((), (), s32[]{:S(2)}) async-start(), calls=%async_computation.3 | async-start | bytes 524288 | tf_op jit(solution)/shard_map/psum | solution.py:64
  599.5 356.4 %all-reduce.19.cloned.1.call-start = ((), (), s32[]{:S(2)}) async-start(), calls=%async_computation.4 | async-start | bytes 524288 | tf_op jit(solution)/shard_map/psum | solution.py:53
  820.9 250.6 %all-reduce.21.cloned.1.call-start = ((), (), s32[]{:S(2)}) async-start(), calls=%async_computation.5 | async-start | bytes 524288 | tf_op jit(solution)/shard_map/psum | solution.py:64
  1000.0 356.2 %all-reduce.23.cloned.1.call-start = ((), (), s32[]{:S(2)}) async-start(), calls=%async_computation.6 | async-start | bytes 524288 | tf_op jit(solution)/shard_map/psum | solution.py:53
  1221.3 250.1 %all-reduce.25.cloned.1.call-start = ((), (), s32[]{:S(2)}) async-start(), calls=%async_computation.7 | async-start | bytes 524288 | tf_op jit(solution)/shard_map/psum | solution.py:64
  1399.8 356.4 %all-reduce.27.cloned.1.call-start = ((), (), s32[]{:S(2)}) async-start(), calls=%async_computation.8 | async-start | bytes 524288 | tf_op jit(solution)/shard_map/psum | solution.py:53
  1621.4 250.1 %all-reduce.29.cloned.1.call-start = ((), (), s32[]{:S(2)}) async-start(), calls=%async_computation.9 | async-start | bytes 524288 | tf_op jit(solution)/shard_map/psum | solution.py:64
Sparse Core Ops, SparseCore 0:
  14.8 140.7 all-reduce.10
  199.5 71.3 all-reduce.12
  421.1 134.7 all-reduce.14
  599.7 71.3 all-reduce.16
  821.0 134.9 all-reduce.18
  1000.1 71.3 all-reduce.20
  1221.4 134.7 all-reduce.22
  1400.0 71.3 all-reduce.24
  1621.5 134.7 all-reduce.26
  1800.5 70.9 all-reduce.28
